TPU v7x, 32 devices: a whole 2x2x4 slice. The times are simulated.
32 devices in a mesh: blk: 8 (over z, core), tenant: 4 (over y, x).
Axes of the slice: x: 2, y: 2, z: 4, core: 2. Of those that a mesh axis runs over, the one named last changes fastest.
Arguments:
- history_u: bfloat16 [4, 1024, 4096], P('tenant', 'blk'), may hold values from -6 to 6
- span_gate: bfloat16 [4, 64, 4096], P('tenant', 'blk'), may hold values from -6 to 6
- span_key: bfloat16 [4, 64, 4096], P('tenant', 'blk'), may hold values from -6 to 6
- span_value: bfloat16 [4, 64, 4096], P('tenant', 'blk'), may hold values from -6 to 6
- filter_taps: bfloat16 [1088, 256], P(('blk', 'tenant'))
- skip_bias: bfloat16 [4096], P(('blk', 'tenant')), may hold values from -6 to 6
- lengths: int32 [4], P('tenant'), may hold values from 1 to 1024, as said below
- page_owner: int32 [4, 8, 1], P('tenant'), may hold values from 0 to 7; in each aligned block of 8 rows (0 to 7, 8 to 15, ..., all dimensions but the last counted through in order) at most 2 rows name the same one
Outputs:
- mixed: bfloat16 [4, 64, 4096], P('tenant', 'blk')
- new_pool: bfloat16 [4, 128, 4096], P('tenant', 'blk')
Inputs may be any that keep to these rules, and one draw needn't show every extreme that they name: `lengths`: lengths are at least 1, and some tenant uses all 1024 cached positions in every draw. `page_owner`: among the 8 pages of one tenant no device is named more than 2 times, and some device is named exactly 2 times.
All inputs are finite; a program needn't handle non-finite values.
Results may differ from a plain program's by a relative error of at most 0.0044.
Values may be sent and summed in bfloat16 or wider, within the bound.
No kernel may reach another device: no remote copies, remote signals or barrier semaphores. Data moves between devices by JAX's collectives and lax.ppermute only.
A program may use at most 128 MiB of HBM per device.

v0:
```python
import jax
import jax.numpy as jnp
from jax import lax
from jax.sharding import PartitionSpec as P

PAGE = 8
PAGES_DEV = 1
MOST = 2


def toeplitz(window, tile_rows, groups):
    reversed_taps = jnp.transpose(window[::-1])
    repeated = jnp.tile(reversed_taps, (1, tile_rows))
    trimmed = repeated[:, tile_rows - 1 : tile_rows - 1 + tile_rows * (2 * tile_rows - 2)]
    return trimmed.reshape(groups, tile_rows, 2 * tile_rows - 2)[:, :, :tile_rows]


def tile_table(padded_filter, starts, tile_rows, groups):

    def one_window(start):
        window = lax.dynamic_slice_in_dim(padded_filter, start, 2 * tile_rows - 1, 0)
        return toeplitz(window, tile_rows, groups)

    return jax.vmap(one_window)(starts)


def blocked_convolution(table, sources_reversed, target_blocks, source_blocks):

    def per_target(target_index):
        tiles = lax.dynamic_slice_in_dim(table, target_index, source_blocks, 0)
        return jnp.einsum(
            "mgab,mbgc->agc", tiles, sources_reversed, preferred_element_type=jnp.float32
        )

    return lax.map(per_target, jnp.arange(target_blocks, dtype=jnp.int32))


def per_device(
    history_u, span_gate, span_key, span_value, filter_taps, skip_bias, lengths, page_owner
):
    cycle_size = lax.axis_size("blk")
    own_index = lax.axis_index("blk")
    history = history_u[0]
    gate_rows = span_gate[0]
    history_rows, width = history.shape
    span_rows = gate_rows.shape[0]
    span_total = span_rows * cycle_size
    groups = filter_taps.shape[1]
    group_size = width // groups
    taps_all, bias_all = (
        lax.all_gather(filter_taps, ("blk", "tenant"), axis=0, tiled=True),
        lax.all_gather(skip_bias, ("blk", "tenant"), axis=0, tiled=True),
    )
    length = lengths[0]
    own_rows = (span_key[0].astype(jnp.float32) * span_value[0].astype(jnp.float32)).astype(
        jnp.bfloat16
    )
    tile_rows = min(32, history_rows, span_total)
    target_blocks = span_total // tile_rows
    column_history, column_span = (
        lax.all_to_all(history, "blk", split_axis=1, concat_axis=0, tiled=True),
        lax.all_to_all(own_rows, "blk", split_axis=1, concat_axis=0, tiled=True),
    )
    column_width = width // cycle_size
    local_groups = column_width // group_size
    full_rows = column_history.shape[0]
    filter_rows_all = full_rows + span_total
    taps_local = lax.dynamic_slice_in_dim(taps_all, own_index * local_groups, local_groups, 1)
    masked_columns = jnp.where(
        jnp.arange(full_rows, dtype=jnp.int32)[:, None] < length,
        column_history,
        jnp.zeros_like(column_history),
    )
    sequence = jnp.concatenate(
        [masked_columns, jnp.zeros((span_total, column_width), jnp.bfloat16)], axis=0
    )
    sequence = lax.dynamic_update_slice(sequence, column_span, (length, jnp.int32(0)))
    source_blocks = filter_rows_all // tile_rows
    padded_filter = jnp.concatenate(
        [jnp.zeros((filter_rows_all, local_groups), jnp.bfloat16), taps_local], axis=0
    )
    offsets = jnp.arange(target_blocks + source_blocks - 1, dtype=jnp.int32) - (source_blocks - 1)
    starts = length + offsets * tile_rows - (tile_rows - 1) + filter_rows_all
    table = tile_table(padded_filter, starts, tile_rows, local_groups)
    sources_reversed = sequence.reshape(source_blocks, tile_rows, local_groups, group_size)[::-1]
    column_out = blocked_convolution(table, sources_reversed, target_blocks, source_blocks).reshape(
        span_total, column_width
    )
    convolved = lax.all_to_all(column_out, "blk", split_axis=0, concat_axis=1, tiled=True)
    mixed = (
        gate_rows.astype(jnp.float32)
        * (convolved + bias_all.astype(jnp.float32)[None, :] * own_rows.astype(jnp.float32))
    ).astype(jnp.bfloat16)
    owners = page_owner[0, :, 0]
    page_count = owners.shape[0]
    onehot = (owners[:, None] == jnp.arange(cycle_size, dtype=jnp.int32)[None, :]).astype(jnp.int32)
    before = jnp.cumsum(onehot, axis=0) - onehot
    slot_rank = jnp.sum(before * onehot, axis=1)
    selector = (
        (owners[None, :] == own_index)
        & (slot_rank[None, :] == jnp.arange(MOST, dtype=jnp.int32)[:, None])
    ).astype(jnp.bfloat16)
    local_pages = own_rows.reshape(PAGES_DEV, PAGE * width)
    targets_of = lax.dynamic_slice_in_dim(owners, own_index * PAGES_DEV, PAGES_DEV, 0)
    send_mask = targets_of[None, :] == jnp.arange(cycle_size, dtype=jnp.int32)[:, None]
    outgoing = jnp.where(
        send_mask[:, :, None], local_pages[None, :, :], jnp.zeros((), jnp.bfloat16)
    )
    incoming = lax.all_to_all(outgoing, "blk", split_axis=0, concat_axis=0, tiled=True)
    arrived = incoming.reshape(page_count, PAGE * width)
    new_pool = jnp.dot(selector, arrived, preferred_element_type=jnp.float32).astype(jnp.bfloat16)
    return (mixed[None], new_pool.reshape(MOST * PAGE, width)[None])


def solution(mesh):
    return jax.shard_map(
        per_device,
        mesh=mesh,
        in_specs=(
            P("tenant", "blk", None),
            P("tenant", "blk", None),
            P("tenant", "blk", None),
            P("tenant", "blk", None),
            P(("blk", "tenant"), None),
            P(("blk", "tenant")),
            P("tenant"),
            P("tenant", None, None),
        ),
        out_specs=(P("tenant", "blk", None), P("tenant", "blk", None)),
        check_vma=False,
    )
```

profile of v0, /device:TPU:0, one launch (start us, length us, event | category | flops | bytes accessed | tf_op | source)
XLA Modules:
  0.0 384.5 jit_solution(1890351494734139457)
XLA Ops:
  0.6 1.3 constant_dynamic-slice_fusion.1
  2.6 1.5 multiply_convert_fusion.1
  6.5 3.8 reduce
  11.4 6.3 %all-to-all-start.3 = ((bf16[8,2,16384]{2,1,0:T(2,128)(2,1)}), bf16[8,2,16384]{2,1,0:T(2,128)(2,1)S(1)}, u32[]{:S(2)}, u32[]{:S(2)}) async-start(bf16[8,2,16384]{2,1,0:T(2,128)(2,1)} %reshape.183), calls=%async_computation.3 | async-start | bytes 1048576 | tf_op jit(solution)/shard_map/all_to_all | solution.py:109
  17.8 74.8 %all-gather = bf16[32,34,256]{2,1,0:T(8,128)(2,1)S(1)} all-gather(bf16[1,34,256]{2,1,0:T(8,128)(2,1)} %bitcast.67), channel_id=1, replica_groups=mesh['blk'=8,'tenant'=4] {'blk','tenant'}, dimensions={0}, use_global_device_ids=true | all-gather | bytes 574464 | tf_op jit(solution)/shard_map/all_gather | solution.py:51
  93.4 1.3 copy.31
  95.0 3.7 all-to-all-start
  98.8 65.2 %while.12 = (s32[]{:T(128)}, bf16[2176,32]{1,0:T(8,128)(2,1)S(1)}, s32[35,2]{0,1:T(2,128)S(1)}, bf16[35,63,32]{2,1,0:T(8,128)(2,1)}, s32[]{:T(128)}) while((s32[]{:T(128)}, bf16[2176,32]{1,0:T(8,128)(2,1)S(1)}, s32[35,2]{0,1:T(2,128)S(1)}, bf16[35,63,32]{2,1,0:T(8,128)(2,1)}, s32[]{:T(128)}) %tuple.37), condition=%wide.while_cond, body=%wide.while_body.sunk | while | flops 2 | bytes 21529 | solution.py:21
  106.8 1.3 bitcast_dynamic-update-slice_fusion.2
  112.4 1.3 bitcast_dynamic-update-slice_fusion.2
  119.9 1.3 bitcast_dynamic-update-slice_fusion.2
  127.3 1.3 bitcast_dynamic-update-slice_fusion.2
  149.7 1.3 bitcast_dynamic-update-slice_fusion.2
  164.0 2.3 rev.6
  166.6 4.7 %tile.4 = bf16[35,32,32,63]{3,2,1,0:T(8,128)(2,1)} broadcast(bf16[35,32,63]{2,1,0:T(8,128)(2,1)S(1)} %copy.30), dimensions={0,1,3} | broadcast | bytes 4656960 | tf_op jit(solution)/shard_map/vmap()/tile | solution.py:13
  171.3 16.1 %tile.10 = bf16[35,32,2016]{2,1,0:T(8,128)(2,1)} reshape(bf16[35,32,32,63]{3,2,1,0:T(8,128)(2,1)} %tile.4) | data formatting | bytes 9031680 | tf_op jit(solution)/shard_map/vmap()/tile | solution.py:13
  187.4 6.9 %slice.19 = bf16[35,32,1984]{2,1,0:T(8,128)(2,1)} slice(bf16[35,32,2016]{2,1,0:T(8,128)(2,1)} %tile.10), slice={[0:35], [0:32], [31:2015]} | slice | bytes 8888320 | tf_op jit(solution)/shard_map/vmap()/slice | solution.py:14
  194.4 31.4 %reshape.155 = bf16[35,32,32,62]{3,2,1,0:T(8,128)(2,1)} reshape(bf16[35,32,1984]{2,1,0:T(8,128)(2,1)} %slice.19) | data formatting | bytes 8888320 | tf_op jit(solution)/shard_map/vmap()/reshape | solution.py:15
  225.8 14.3 %copy.34 = bf16[35,32,32,32]{0,2,3,1:T(8,128)(2,1)} copy(bf16[35,32,32,32]{3,2,1,0:T(8,128)(2,1)} %bitcast.60) | data formatting | bytes 4587520 | tf_op jit(solution)/shard_map/while | solution.py:35
  240.1 66.1 %all-gather.1 = bf16[32,1,128]{2,1,0:T(2,128)(2,1)S(1)} all-gather(bf16[1,1,128]{2,1,0:T(2,128)(2,1)S(1)} %bitcast.70), channel_id=1, replica_groups=mesh['blk'=8,'tenant'=4] {'blk','tenant'}, dimensions={0}, use_global_device_ids=true | all-gather | bytes 8448 | tf_op jit(solution)/shard_map/all_gather | solution.py:52
  307.1 3.6 all-to-all-start.1
  311.5 4.8 %all-to-all-done.1 = bf16[8,8,512]{2,0,1:T(8,128)(2,1)S(1)} async-done(((bf16[8,8,512]{2,0,1:T(8,128)(2,1)}), bf16[8,8,512]{2,0,1:T(8,128)(2,1)S(1)}, u32[]{:S(2)}, u32[]{:S(2)}) %all-to-all-start.1) | async-done | bytes 65568 | tf_op jit(solution)/shard_map/all_to_all | solution.py:62
  317.4 4.8 %reshape.156 = bf16[34,32,32,16]{1,0,3,2:T(8,128)(2,1)} reshape(bf16[1088,512]{0,1:T(8,128)(2,1)S(1)} %copy.33) | data formatting | bytes 2228224 | tf_op jit(solution)/shard_map/reshape | solution.py:85
  322.2 20.3 %rev.7 = bf16[34,32,32,16]{1,0,3,2:T(8,128)(2,1)} reverse(bf16[34,32,32,16]{1,0,3,2:T(8,128)(2,1)} %reshape.156), dimensions={0} | reverse | bytes 2228224 | tf_op jit(solution)/shard_map/rev | solution.py:85
  342.5 8.7 %copy.35 = bf16[34,32,32,16]{0,3,1,2:T(8,128)(2,1)} copy(bf16[34,32,32,16]{1,0,3,2:T(8,128)(2,1)} %rev.7) | data formatting | bytes 2228224 | tf_op jit(solution)/shard_map/while | solution.py:35
  351.2 19.5 %while.11 = (s32[]{:T(128)}, f32[2,32,32,16]{1,3,2,0:T(8,128)S(1)}, s32[2]{0:T(128)S(1)}, bf16[35,32,32,32]{0,2,3,1:T(8,128)(2,1)}, bf16[34,32,32,16]{0,3,1,2:T(8,128)(2,1)}, /*index=5*/s32[]{:T(128)}, s32[]{:T(128)}, s32[]{:T(128)}) while((s32[]{:T(128)}, f32[2,32,32,16]{1,3,2,0:T(8,128)S(1)}, s32[2]{0:T(128)S(1)}, ...), condition=%wide.region_1.2_spmd, body=%wide.region_0.1_spmd.sunk | while | flops 35651588 | bytes 3670155 | solution.py:35
  354.0 7.0 %fusion.23 = f32[2,32,32,16]{1,3,2,0:T(8,128)S(1)} fusion(f32[2,32,32,16]{1,3,2,0:T(8,128)S(1)} %get-tuple-element.156, s32[]{:T(128)} %get-tuple-element.155, bf16[34,32,32,16]{0,3,1,2:T(8,128)(2,1)} %get-tuple-element.167, bf16[35,32,32,32]{0,2,3,1:T(8,128)(2,1)} %get-tuple-element.166, s32[]{:T(128)S(6)} %select_n.48), kind=kOutput, calls=%fused_computation.3.clone.1 | convolution fusion | flops 35651584 | bytes 3670024 | tf_op jit(solution)/shard_map/while/body/eval_jaxpr/mgab,mbgc->agc/dot_general | solution.py:31
  363.7 7.0 %fusion.23 = f32[2,32,32,16]{1,3,2,0:T(8,128)S(1)} fusion(f32[2,32,32,16]{1,3,2,0:T(8,128)S(1)} %get-tuple-element.156, s32[]{:T(128)} %get-tuple-element.155, bf16[34,32,32,16]{0,3,1,2:T(8,128)(2,1)} %get-tuple-element.167, bf16[35,32,32,32]{0,2,3,1:T(8,128)(2,1)} %get-tuple-element.166, s32[]{:T(128)S(6)} %select_n.48), kind=kOutput, calls=%fused_computation.3.clone.1 | convolution fusion | flops 35651584 | bytes 3670024 | tf_op jit(solution)/shard_map/while/body/eval_jaxpr/mgab,mbgc->agc/dot_general | solution.py:31
  371.6 1.3 all_to_all.50
  372.9 3.4 all-to-all-start.2
  377.7 5.3 %all-to-all-done.2 = f32[8,8,512]{2,1,0:T(8,128)S(1)} async-done(((f32[8,8,512]{2,1,0:T(8,128)}), f32[8,8,512]{2,1,0:T(8,128)S(1)}, u32[]{:S(2)}, u32[]{:S(2)}) %all-to-all-start.2) | async-done | bytes 131104 | tf_op jit(solution)/shard_map/all_to_all | solution.py:89
  383.0 1.5 multiply_convert_fusion
  (143 shorter events, 70.2 us)
Async XLA Ops:
  0.6 92.8 %copy-start = (bf16[1,128,4096]{2,1,0:T(8,128)(2,1)S(1)}, bf16[1,128,4096]{2,1,0:T(8,128)(2,1)}, u32[]{:S(2)}) copy-start(bf16[1,128,4096]{2,1,0:T(8,128)(2,1)} %param.10) | copy-start | bytes 3145732
  11.4 83.6 %all-to-all-start.3 = ((bf16[8,2,16384]{2,1,0:T(2,128)(2,1)}), bf16[8,2,16384]{2,1,0:T(2,128)(2,1)S(1)}, u32[]{:S(2)}, u32[]{:S(2)}) async-start(bf16[8,2,16384]{2,1,0:T(2,128)(2,1)} %reshape.183), calls=%async_computation.3 | async-start | bytes 1048576 | tf_op jit(solution)/shard_map/all_to_all | solution.py:109
  95.0 212.0 %all-to-all-start = ((bf16[128,8,512]{0,2,1:T(8,128)(2,1)}), bf16[128,8,512]{0,2,1:T(8,128)(2,1)S(1)}, u32[]{:S(2)}, u32[]{:S(2)}) async-start(bf16[128,8,512]{0,2,1:T(8,128)(2,1)} %bitcast.8), calls=%async_computation | async-start | bytes 2097152 | tf_op jit(solution)/shard_map/all_to_all | solution.py:61
  225.8 14.3 %copy-start.4 = (bf16[128]{0:T(256)(128)(2,1)S(1)}, bf16[128]{0:T(256)(128)(2,1)}, u32[]{:S(2)}) copy-start(bf16[128]{0:T(256)(128)(2,1)} %param.15) | copy-start | bytes 772
  225.8 80.4 %copy-start.3 = (s32[1,8,1]{1,2,0:T(1,128)S(1)}, s32[1,8,1]{1,2,0:T(1,128)}, u32[]{:S(2)}) copy-start(s32[1,8,1]{1,2,0:T(1,128)} %param.17) | copy-start | bytes 100
  307.1 9.2 %all-to-all-start.1 = ((bf16[8,8,512]{2,0,1:T(8,128)(2,1)}), bf16[8,8,512]{2,0,1:T(8,128)(2,1)S(1)}, u32[]{:S(2)}, u32[]{:S(2)}) async-start(bf16[8,8,512]{2,0,1:T(8,128)(2,1)} %bitcast.11), calls=%async_computation.1 | async-start | bytes 131072 | tf_op jit(solution)/shard_map/all_to_all | solution.py:62
  342.5 8.7 %copy-start.1 = (f32[2,32,32,16]{1,3,2,0:T(8,128)S(1)}, f32[2,32,32,16]{1,3,2,0:T(8,128)}, u32[]{:S(2)}) copy-start(f32[2,32,32,16]{1,3,2,0:T(8,128)} %custom-call) | copy-start | bytes 393220
  351.2 31.8 %copy-start.2 = (bf16[1,8,4096]{2,1,0:T(8,128)(2,1)S(1)}, bf16[1,8,4096]{2,1,0:T(8,128)(2,1)}, u32[]{:S(2)}) copy-start(bf16[1,8,4096]{2,1,0:T(8,128)(2,1)} %param.11) | copy-start | bytes 196612
  372.9 10.1 %all-to-all-start.2 = ((f32[8,8,512]{2,1,0:T(8,128)}), f32[8,8,512]{2,1,0:T(8,128)S(1)}, u32[]{:S(2)}, u32[]{:S(2)}) async-start(f32[8,8,512]{2,1,0:T(8,128)} %all_to_all.50), calls=%async_computation.2 | async-start | bytes 262144 | tf_op jit(solution)/shard_map/all_to_all | solution.py:89
where the time goes:
time: 387 us; the launch traced here: 385 us
  local copies, waits for them, and re-layouts  187 us (48%)
  blocking collectives  141 us (36%)
  starting transfers between devices  17 us (4%)
  matrix products  14.7 us (4%)
  waiting for transfers between devices  10.1 us (3%)
  other arithmetic  8.95 us (2%)
  loops' own time  4.23 us (1%)
    all_gather x1, blocking collectives, per_device(): lax.all_gather(filter_taps, ('blk', 'tenant'), axis=0, tiled=True)  74.8 us
    all_gather x1, blocking collectives, per_device(): lax.all_gather(skip_bias, ('blk', 'tenant'), axis=0, tiled=True)  66.1 us
    gather x105, local copies, waits for them, and re-layouts  65.1 us
    reshape x1, local copies, waits for them, and re-layouts, toeplitz(): trimmed.reshape(groups, tile_rows, 2 * tile_rows - 2)[:, :, :tile_rows]  31.4 us
    while x3, local copies, waits for them, and re-layouts, blocked_convolution(): return lax.map(per_target, jnp.arange(target_blocks, dtype=jnp.int32))  23.9 us
    another operation x2, local copies, waits for them, and re-layouts, toeplitz(): repeated = jnp.tile(reversed_taps, (1, tile_rows))  20.8 us
    rev x1, local copies, waits for them, and re-layouts, per_device(): sequence.reshape(source_blocks, tile_rows, local_groups, group_size)[::-1]  20.3 us
    dot_general x2, matrix products, per_target(): jnp.einsum('mgab,mbgc->agc', tiles, sources_reversed, preferred_element_t...  14 us
  transfers between devices with their start and end apart: 4, of which 2 were waited for; matrix products, arithmetic and copies ran while one was open for 38% of the time, Pallas kernels for 0%

commit v1 on v0

--- a/solution.py
+++ b/solution.py
@@ -86,7 +86,9 @@
     column_out = blocked_convolution(table, sources_reversed, target_blocks, source_blocks).reshape(
         span_total, column_width
     )
-    convolved = lax.all_to_all(column_out, "blk", split_axis=0, concat_axis=1, tiled=True)
+    pieces = jnp.split(column_out, lax.axis_size("blk"), axis=0)
+    received = lax.all_to_all(jnp.stack(pieces), "blk", 0, 0)
+    convolved = jnp.concatenate(received, axis=1)
     mixed = (
         gate_rows.astype(jnp.float32)
         * (convolved + bias_all.astype(jnp.float32)[None, :] * own_rows.astype(jnp.float32))

time: 387 us -> 400 us (1.034)
  local copies, waits for them, and re-layouts: 187 us -> 201 us
    dynamic_update_slice x0 -> x2, local copies, waits for them, and re-layouts: none -> 11 us  [blocked_convolution(): return lax.map(per_target, jnp.arange(target_blocks, dtype=jnp.int32))]
    unnamed x15 -> x22, local copies, waits for them, and re-layouts: 4.04 us -> 8.28 us
    while x3 -> x2, local copies, waits for them, and re-layouts: 23.9 us -> 23 us  [blocked_convolution(): return lax.map(per_target, jnp.arange(target_blocks, dtype=jnp.int32))]
  transfers between devices with their start and end apart: 4 -> 4, of which waited for: 2 -> 2; matrix products, arithmetic and copies ran while one was open for 38% -> 36% of each run, Pallas kernels for 0% -> 0%
where the time goes in v1:
time: 400 us; the launch traced here: 398 us
  local copies, waits for them, and re-layouts  201 us (50%)
  blocking collectives  141 us (35%)
  starting transfers between devices  17 us (4%)
  matrix products  14.7 us (4%)
  waiting for transfers between devices  10.1 us (3%)
  other arithmetic  8.95 us (2%)
    all_gather x1, blocking collectives, per_device(): lax.all_gather(filter_taps, ('blk', 'tenant'), axis=0, tiled=True)  74.8 us
    all_gather x1, blocking collectives, per_device(): lax.all_gather(skip_bias, ('blk', 'tenant'), axis=0, tiled=True)  66.1 us
    gather x105, local copies, waits for them, and re-layouts  62.4 us
    reshape x1, local copies, waits for them, and re-layouts, toeplitz(): trimmed.reshape(groups, tile_rows, 2 * tile_rows - 2)[:, :, :tile_rows]  31.4 us
    while x2, local copies, waits for them, and re-layouts, blocked_convolution(): return lax.map(per_target, jnp.arange(target_blocks, dtype=jnp.int32))  23 us
    another operation x2, local copies, waits for them, and re-layouts, toeplitz(): repeated = jnp.tile(reversed_taps, (1, tile_rows))  20.9 us
    rev x1, local copies, waits for them, and re-layouts, per_device(): sequence.reshape(source_blocks, tile_rows, local_groups, group_size)[::-1]  20.3 us
    dot_general x2, matrix products, per_target(): jnp.einsum('mgab,mbgc->agc', tiles, sources_reversed, preferred_element_t...  14 us
  transfers between devices with their start and end apart: 4, of which 2 were waited for; matrix products, arithmetic and copies ran while one was open for 36% of the time, Pallas kernels for 0%

profile of v1, /device:TPU:0, one launch (start us, length us, event | category | flops | bytes accessed | tf_op | source)
XLA Modules:
  0.0 397.7 jit_solution(7861492185933958684)
XLA Ops:
  0.6 1.3 constant_dynamic-slice_fusion.1
  2.6 1.5 multiply_convert_fusion.1
  6.5 3.8 reduce
  11.4 6.3 %all-to-all-start.3 = ((bf16[8,2,16384]{2,1,0:T(2,128)(2,1)}), bf16[8,2,16384]{2,1,0:T(2,128)(2,1)S(1)}, u32[]{:S(2)}, u32[]{:S(2)}) async-start(bf16[8,2,16384]{2,1,0:T(2,128)(2,1)} %reshape.190), calls=%async_computation.3 | async-start | bytes 1048576 | tf_op jit(solution)/shard_map/all_to_all | solution.py:111
  17.8 74.8 %all-gather = bf16[32,34,256]{2,1,0:T(8,128)(2,1)S(1)} all-gather(bf16[1,34,256]{2,1,0:T(8,128)(2,1)} %bitcast.83), channel_id=1, replica_groups=mesh['blk'=8,'tenant'=4] {'blk','tenant'}, dimensions={0}, use_global_device_ids=true | all-gather | bytes 574464 | tf_op jit(solution)/shard_map/all_gather | solution.py:51
  93.4 1.3 copy.41
  95.0 3.7 all-to-all-start
  98.8 62.4 %while.12 = (s32[]{:T(128)}, bf16[2176,32]{1,0:T(8,128)(2,1)S(1)}, s32[35,2]{0,1:T(2,128)S(1)}, bf16[35,63,32]{2,1,0:T(8,128)(2,1)}, s32[]{:T(128)}) while((s32[]{:T(128)}, bf16[2176,32]{1,0:T(8,128)(2,1)S(1)}, s32[35,2]{0,1:T(2,128)S(1)}, bf16[35,63,32]{2,1,0:T(8,128)(2,1)}, s32[]{:T(128)}) %tuple.44), condition=%wide.while_cond, body=%wide.while_body.sunk | while | flops 2 | bytes 21529 | solution.py:21
  104.7 1.2 bitcast_dynamic-update-slice_fusion.2
  110.1 1.2 bitcast_dynamic-update-slice_fusion.2
  124.3 1.2 bitcast_dynamic-update-slice_fusion.2
  145.8 1.2 bitcast_dynamic-update-slice_fusion.2
  161.2 2.3 rev.6
  163.8 4.7 %tile.4 = bf16[35,32,32,63]{3,2,1,0:T(8,128)(2,1)} broadcast(bf16[35,32,63]{2,1,0:T(8,128)(2,1)S(1)} %copy.40), dimensions={0,1,3} | broadcast | bytes 4656960 | tf_op jit(solution)/shard_map/vmap()/tile | solution.py:13
  168.6 16.1 %tile.10 = bf16[35,32,2016]{2,1,0:T(8,128)(2,1)} reshape(bf16[35,32,32,63]{3,2,1,0:T(8,128)(2,1)} %tile.4) | data formatting | bytes 9031680 | tf_op jit(solution)/shard_map/vmap()/tile | solution.py:13
  184.7 6.9 %slice.19 = bf16[35,32,1984]{2,1,0:T(8,128)(2,1)} slice(bf16[35,32,2016]{2,1,0:T(8,128)(2,1)} %tile.10), slice={[0:35], [0:32], [31:2015]} | slice | bytes 8888320 | tf_op jit(solution)/shard_map/vmap()/slice | solution.py:14
  191.6 31.4 %reshape.159 = bf16[35,32,32,62]{3,2,1,0:T(8,128)(2,1)} reshape(bf16[35,32,1984]{2,1,0:T(8,128)(2,1)} %slice.19) | data formatting | bytes 8888320 | tf_op jit(solution)/shard_map/vmap()/reshape | solution.py:15
  223.0 14.3 %copy.44 = bf16[35,32,32,32]{0,2,3,1:T(8,128)(2,1)} copy(bf16[35,32,32,32]{3,2,1,0:T(8,128)(2,1)} %bitcast.75) | data formatting | bytes 4587520 | tf_op jit(solution)/shard_map/while | solution.py:35
  237.3 66.1 %all-gather.1 = bf16[32,1,128]{2,1,0:T(2,128)(2,1)S(1)} all-gather(bf16[1,1,128]{2,1,0:T(2,128)(2,1)S(1)} %bitcast.86), channel_id=1, replica_groups=mesh['blk'=8,'tenant'=4] {'blk','tenant'}, dimensions={0}, use_global_device_ids=true | all-gather | bytes 8448 | tf_op jit(solution)/shard_map/all_gather | solution.py:52
  304.3 3.6 all-to-all-start.1
  308.7 4.8 %all-to-all-done.1 = bf16[8,8,512]{2,0,1:T(8,128)(2,1)S(1)} async-done(((bf16[8,8,512]{2,0,1:T(8,128)(2,1)}), bf16[8,8,512]{2,0,1:T(8,128)(2,1)S(1)}, u32[]{:S(2)}, u32[]{:S(2)}) %all-to-all-start.1) | async-done | bytes 65568 | tf_op jit(solution)/shard_map/all_to_all | solution.py:62
  314.6 4.8 %reshape.160 = bf16[34,32,32,16]{1,0,3,2:T(8,128)(2,1)} reshape(bf16[1088,512]{0,1:T(8,128)(2,1)S(1)} %copy.43) | data formatting | bytes 2228224 | tf_op jit(solution)/shard_map/reshape | solution.py:85
  319.4 20.3 %rev.7 = bf16[34,32,32,16]{1,0,3,2:T(8,128)(2,1)} reverse(bf16[34,32,32,16]{1,0,3,2:T(8,128)(2,1)} %reshape.160), dimensions={0} | reverse | bytes 2228224 | tf_op jit(solution)/shard_map/rev | solution.py:85
  339.7 8.7 %copy.45 = bf16[34,32,32,16]{0,3,1,2:T(8,128)(2,1)} copy(bf16[34,32,32,16]{1,0,3,2:T(8,128)(2,1)} %rev.7) | data formatting | bytes 2228224 | tf_op jit(solution)/shard_map/while | solution.py:35
  348.4 29.6 %while.11 = (s32[]{:T(128)}, f32[2,32,32,16]{1,0,3,2:T(2,128)S(1)}, s32[2]{0:T(128)S(1)}, bf16[35,32,32,32]{0,2,3,1:T(8,128)(2,1)}, bf16[34,32,32,16]{0,3,1,2:T(8,128)(2,1)}, /*index=5*/s32[]{:T(128)}, s32[]{:T(128)}, s32[]{:T(128)}) while((s32[]{:T(128)}, f32[2,32,32,16]{1,0,3,2:T(2,128)S(1)}, s32[2]{0:T(128)S(1)}, ...), condition=%wide.region_1.2_spmd, body=%wide.region_0.1_spmd.sunk | while | flops 35651588 | bytes 3604619 | solution.py:35
  350.7 7.0 %fusion.17 = f32[32,32,16,1]{1,2,3,0:T(8,128)S(1)} fusion(bf16[34,32,32,16]{0,3,1,2:T(8,128)(2,1)} %get-tuple-element.175, bf16[35,32,32,32]{0,2,3,1:T(8,128)(2,1)} %get-tuple-element.174, s32[]{:T(128)S(6)} %select_n.48), kind=kOutput, calls=%fused_computation.clone.1 | convolution fusion | flops 35651584 | bytes 3473412 | tf_op jit(solution)/shard_map/while/body/eval_jaxpr/mgab,mbgc->agc/dot_general | solution.py:31
  357.7 5.5 %dynamic_update_slice.9 = f32[2,32,32,16]{1,0,3,2:T(2,128)S(1)} dynamic-update-slice(f32[2,32,32,16]{1,0,3,2:T(2,128)S(1)} %get-tuple-element.164, f32[1,32,32,16]{1,0,3,2:T(1,128)S(1)} %bitcast.76, s32[]{:T(128)} %get-tuple-element.163, s32[]{:T(128)} %constant.20.clone.1..sunk, s32[]{:T(128)} %constant.20.clone.1..sunk, s32[]{:T(128)} %constant.20.clone.1..sunk) | dynamic-update-slice | bytes 131076 | tf_op jit(solution)/shard_map/while/body/jit(dynamic_update_index_in_dim)/dynamic_update_slice | solution.py:35
  365.5 7.0 %fusion.17 = f32[32,32,16,1]{1,2,3,0:T(8,128)S(1)} fusion(bf16[34,32,32,16]{0,3,1,2:T(8,128)(2,1)} %get-tuple-element.175, bf16[35,32,32,32]{0,2,3,1:T(8,128)(2,1)} %get-tuple-element.174, s32[]{:T(128)S(6)} %select_n.48), kind=kOutput, calls=%fused_computation.clone.1 | convolution fusion | flops 35651584 | bytes 3473412 | tf_op jit(solution)/shard_map/while/body/eval_jaxpr/mgab,mbgc->agc/dot_general | solution.py:31
  372.5 5.5 %dynamic_update_slice.9 = f32[2,32,32,16]{1,0,3,2:T(2,128)S(1)} dynamic-update-slice(f32[2,32,32,16]{1,0,3,2:T(2,128)S(1)} %get-tuple-element.164, f32[1,32,32,16]{1,0,3,2:T(1,128)S(1)} %bitcast.76, s32[]{:T(128)} %get-tuple-element.163, s32[]{:T(128)} %constant.20.clone.1..sunk, s32[]{:T(128)} %constant.20.clone.1..sunk, s32[]{:T(128)} %constant.20.clone.1..sunk) | dynamic-update-slice | bytes 131076 | tf_op jit(solution)/shard_map/while/body/jit(dynamic_update_index_in_dim)/dynamic_update_slice | solution.py:35
  386.1 3.4 all-to-all-start.2
  390.9 5.3 %all-to-all-done.2 = f32[8,8,512]{2,1,0:T(8,128)S(1)} async-done(((f32[8,8,512]{2,1,0:T(8,128)}), f32[8,8,512]{2,1,0:T(8,128)S(1)}, u32[]{:S(2)}, u32[]{:S(2)}) %all-to-all-start.2) | async-done | bytes 131104 | tf_op jit(solution)/shard_map/all_to_all | solution.py:90
  396.2 1.5 multiply_convert_fusion
  (161 shorter events, 75.9 us)
Async XLA Ops:
  0.6 92.8 %copy-start = (bf16[1,128,4096]{2,1,0:T(8,128)(2,1)S(1)}, bf16[1,128,4096]{2,1,0:T(8,128)(2,1)}, u32[]{:S(2)}) copy-start(bf16[1,128,4096]{2,1,0:T(8,128)(2,1)} %param.10) | copy-start | bytes 3145732
  11.4 83.6 %all-to-all-start.3 = ((bf16[8,2,16384]{2,1,0:T(2,128)(2,1)}), bf16[8,2,16384]{2,1,0:T(2,128)(2,1)S(1)}, u32[]{:S(2)}, u32[]{:S(2)}) async-start(bf16[8,2,16384]{2,1,0:T(2,128)(2,1)} %reshape.190), calls=%async_computation.3 | async-start | bytes 1048576 | tf_op jit(solution)/shard_map/all_to_all | solution.py:111
  95.0 209.3 %all-to-all-start = ((bf16[128,8,512]{0,2,1:T(8,128)(2,1)}), bf16[128,8,512]{0,2,1:T(8,128)(2,1)S(1)}, u32[]{:S(2)}, u32[]{:S(2)}) async-start(bf16[128,8,512]{0,2,1:T(8,128)(2,1)} %bitcast.8), calls=%async_computation | async-start | bytes 2097152 | tf_op jit(solution)/shard_map/all_to_all | solution.py:61
  223.0 14.3 %copy-start.4 = (bf16[128]{0:T(256)(128)(2,1)S(1)}, bf16[128]{0:T(256)(128)(2,1)}, u32[]{:S(2)}) copy-start(bf16[128]{0:T(256)(128)(2,1)} %param.15) | copy-start | bytes 772
  223.0 80.4 %copy-start.3 = (s32[1,8,1]{1,2,0:T(1,128)S(1)}, s32[1,8,1]{1,2,0:T(1,128)}, u32[]{:S(2)}) copy-start(s32[1,8,1]{1,2,0:T(1,128)} %param.17) | copy-start | bytes 100
  304.3 9.2 %all-to-all-start.1 = ((bf16[8,8,512]{2,0,1:T(8,128)(2,1)}), bf16[8,8,512]{2,0,1:T(8,128)(2,1)S(1)}, u32[]{:S(2)}, u32[]{:S(2)}) async-start(bf16[8,8,512]{2,0,1:T(8,128)(2,1)} %bitcast.11), calls=%async_computation.1 | async-start | bytes 131072 | tf_op jit(solution)/shard_map/all_to_all | solution.py:62
  339.7 8.7 %copy-start.1 = (f32[2,32,32,16]{1,0,3,2:T(2,128)S(1)}, f32[2,32,32,16]{1,0,3,2:T(2,128)}, u32[]{:S(2)}) copy-start(f32[2,32,32,16]{1,0,3,2:T(2,128)} %custom-call.1) | copy-start | bytes 393220
  378.0 18.2 %copy-start.2 = (bf16[1,8,4096]{2,1,0:T(8,128)(2,1)S(1)}, bf16[1,8,4096]{2,1,0:T(8,128)(2,1)}, u32[]{:S(2)}) copy-start(bf16[1,8,4096]{2,1,0:T(8,128)(2,1)} %param.11) | copy-start | bytes 196612
  386.1 10.1 %all-to-all-start.2 = ((f32[8,8,512]{2,1,0:T(8,128)}), f32[8,8,512]{2,1,0:T(8,128)S(1)}, u32[]{:S(2)}, u32[]{:S(2)}) async-start(f32[8,8,512]{2,1,0:T(8,128)} %constant_dynamic-update-slice_fusion), calls=%async_computation.2 | async-start | bytes 262144 | tf_op jit(solution)/shard_map/all_to_all | solution.py:90
